TPU v7x, 32 devices: a whole 2x2x4 slice. The times are simulated.
32 devices in a mesh: ctx: 8 (over y, x, core), fsdp: 4 (over z).
Axes of the slice: x: 2, y: 2, z: 4, core: 2. Of those that a mesh axis runs over, the one named last changes fastest.
Arguments:
- tokens_in: bfloat16 [4, 1024, 1024], P('fsdp', 'ctx'), may hold values from -6 to 6
- doc_lengths: int32 [4, 8], P('fsdp'), may hold values from 1 to 512, 1024 in all within a row
- norm1_gain: bfloat16 [1024], P('fsdp'), may hold values from 0.5 to 1.5
- norm1_bias: bfloat16 [1024], P('fsdp'), may hold values from -1.5 to 1.5
- qkv_weight: bfloat16 [1024, 3072], P('fsdp'), may hold values from -0.1875 to 0.1875
- qv_bias: bfloat16 [2048], P('fsdp'), may hold values from -1.5 to 1.5
- out_weight: bfloat16 [1024, 1024], P('fsdp'), may hold values from -1.5 to 1.5
- out_bias: bfloat16 [1024], P('fsdp'), may hold values from -1.5 to 1.5
- norm2_gain: bfloat16 [1024], P('fsdp'), may hold values from 0.5 to 1.5
- norm2_bias: bfloat16 [1024], P('fsdp'), may hold values from -1.5 to 1.5
- up_weight: bfloat16 [1024, 4096], P('fsdp'), may hold values from -0.1875 to 0.1875
- up_bias: bfloat16 [4096], P('fsdp'), may hold values from -1.5 to 1.5
- down_weight: bfloat16 [4096, 1024], P('fsdp'), may hold values from -0.09375 to 0.09375
- down_bias: bfloat16 [1024], P('fsdp'), may hold values from -1.5 to 1.5
- out_cotangent: bfloat16 [4, 1024, 1024], P('fsdp', 'ctx'), may hold values from -6 to 6
Outputs:
- layer_out: bfloat16 [4, 1024, 1024], P('fsdp', 'ctx')
- input_grad: bfloat16 [4, 1024, 1024], P('fsdp', 'ctx')
- norm1_gain_grad: float32 [1024], P(('ctx', 'fsdp'))
- norm1_bias_grad: float32 [1024], P(('ctx', 'fsdp'))
- qkv_weight_grad: float32 [1024, 3072], P(('ctx', 'fsdp'))
- qv_bias_grad: float32 [2048], P(('ctx', 'fsdp'))
- out_weight_grad: float32 [1024, 1024], P(('ctx', 'fsdp'))
- out_bias_grad: float32 [1024], P(('ctx', 'fsdp'))
- norm2_gain_grad: float32 [1024], P(('ctx', 'fsdp'))
- norm2_bias_grad: float32 [1024], P(('ctx', 'fsdp'))
- up_weight_grad: float32 [1024, 4096], P(('ctx', 'fsdp'))
- up_bias_grad: float32 [4096], P(('ctx', 'fsdp'))
- down_weight_grad: float32 [4096, 1024], P(('ctx', 'fsdp'))
- down_bias_grad: float32 [1024], P(('ctx', 'fsdp'))
Inputs may be any that keep to these rules, and one draw needn't show every extreme that they name: `doc_lengths`: each row lists one stream's documents in order; they sum to 1024; the longest is 512.
All inputs are finite; a program needn't handle non-finite values.
Results may differ from a plain program's by a relative error of at most 0.018.
Values may be sent and summed in bfloat16 or wider, within the bound.
A program may use at most 128 MiB of HBM per device.

v0:
```python
import jax
import jax.numpy as jnp
from jax import lax
from jax.sharding import PartitionSpec as P

HEADS = 16
HEAD_DIM = 64


epsilon = 1e-05
masked_score = -1e30


def passed_along(block, axis, distance):
    devices = range(lax.axis_size(axis))
    route = [(i - distance, i) for i in devices if i - distance in devices]
    return lax.ppermute(block, axis, route)


def from_behind(x, axis, by):
    size = lax.axis_size(axis)
    return lax.ppermute(x, axis, [(i, (i + by) % size) for i in range(size)])


def norm_rows(values, gain, offset):
    centre = values - jnp.mean(values, axis=-1, keepdims=True)
    spread = jnp.mean(centre * centre, axis=-1, keepdims=True)
    return centre * lax.rsqrt(spread + epsilon) * gain + offset


def gelu_tanh(values):
    return jax.nn.gelu(values, approximate=True)


def doc_index(positions, doc_ends):
    return jnp.sum((doc_ends[None, :] <= positions[:, None]).astype(jnp.int32), axis=1)


def shards(
    tokens_in,
    doc_lengths,
    norm1_gain,
    norm1_bias,
    qkv_weight,
    qv_bias,
    out_weight,
    out_bias,
    norm2_gain,
    norm2_bias,
    up_weight,
    up_bias,
    down_weight,
    down_bias,
    out_cotangent,
):
    model_width = tokens_in.shape[2]
    tok_rows = tokens_in.shape[1]
    ctx_count = lax.axis_size("ctx")
    ctx_index = lax.axis_index("ctx")
    score_scale = HEAD_DIM ** (-0.5)
    inputs = tokens_in[0].astype(jnp.float32)
    doc_ends = jnp.cumsum(doc_lengths[0])
    query_pos = ctx_index * tok_rows + jnp.arange(tok_rows, dtype=jnp.int32)
    query_doc = doc_index(query_pos, doc_ends)

    def block_mask(anchor):
        key_pos = anchor * tok_rows + jnp.arange(tok_rows, dtype=jnp.int32)
        key_doc = doc_index(key_pos, doc_ends)
        return (key_pos[None, :] <= query_pos[:, None]) & (key_doc[None, :] == query_doc[:, None])

    attn_set = (
        lax.all_gather(norm1_gain, "fsdp", axis=0, tiled=True),
        lax.all_gather(norm1_bias, "fsdp", axis=0, tiled=True),
        lax.all_gather(qkv_weight, "fsdp", axis=0, tiled=True),
        lax.all_gather(qv_bias, "fsdp", axis=0, tiled=True),
        lax.all_gather(out_weight, "fsdp", axis=0, tiled=True),
        lax.all_gather(out_bias, "fsdp", axis=0, tiled=True),
    )
    gain_one, shift_one, w_qkv, b_qv, w_out, b_out = attn_set
    gain_one_f = gain_one.astype(jnp.float32)
    shift_one_f = shift_one.astype(jnp.float32)
    normed1 = norm_rows(inputs, gain_one_f, shift_one_f).astype(jnp.bfloat16)
    bias_full = jnp.concatenate(
        [b_qv[:model_width], jnp.zeros((model_width,), b_qv.dtype), b_qv[model_width:]]
    ).astype(jnp.float32)
    projected = (jnp.dot(normed1, w_qkv, preferred_element_type=jnp.float32) + bias_full).astype(
        jnp.bfloat16
    )
    queries = projected[:, :model_width].reshape(tok_rows, HEADS, HEAD_DIM)
    keys_own = projected[:, model_width : 2 * model_width].reshape(tok_rows, HEADS, HEAD_DIM)
    values_own = projected[:, 2 * model_width :].reshape(tok_rows, HEADS, HEAD_DIM)

    def attend(carry, keys, values, anchor):
        accum, running_top, running_total = carry
        allowed = block_mask(anchor)
        scores = (
            jnp.einsum("thd,shd->hts", queries, keys, preferred_element_type=jnp.float32)
            * score_scale
        )
        scores = jnp.where(allowed[None], scores, masked_score)
        new_top = jnp.maximum(running_top, jnp.max(scores, axis=2))
        weights = jnp.exp(scores - new_top[:, :, None])
        factor = jnp.exp(running_top - new_top)
        running_total = running_total * factor + jnp.sum(weights, axis=2)
        block_part = jnp.einsum(
            "hts,shd->thd", weights.astype(jnp.bfloat16), values, preferred_element_type=jnp.float32
        )
        accum = accum * factor.T[:, :, None] + block_part
        return (accum, new_top, running_total)

    start_carry = (
        jnp.zeros((tok_rows, HEADS, HEAD_DIM), jnp.float32),
        jnp.full((HEADS, tok_rows), masked_score, jnp.float32),
        jnp.zeros((HEADS, tok_rows), jnp.float32),
    )
    first_carry = attend(start_carry, keys_own, values_own, ctx_index)

    def cycle_forward(cycle_step, state):
        keys, values, carry = state
        keys, values = passed_along((keys, values), "ctx", 1)
        anchor = (ctx_index - cycle_step) % ctx_count
        return (keys, values, attend(carry, keys, values, anchor))

    _, _, final_carry = lax.fori_loop(
        1, ctx_count, cycle_forward, (keys_own, values_own, first_carry)
    )
    accum, running_top, running_total = final_carry
    log_total = running_top + jnp.log(running_total)
    mix = (accum / running_total.T[:, :, None]).reshape(tok_rows, model_width).astype(jnp.bfloat16)
    resid = (
        inputs + jnp.dot(mix, w_out, preferred_element_type=jnp.float32) + b_out.astype(jnp.float32)
    )
    mlp_set = (
        lax.all_gather(norm2_gain, "fsdp", axis=0, tiled=True),
        lax.all_gather(norm2_bias, "fsdp", axis=0, tiled=True),
        lax.all_gather(up_weight, "fsdp", axis=0, tiled=True),
        lax.all_gather(up_bias, "fsdp", axis=0, tiled=True),
        lax.all_gather(down_weight, "fsdp", axis=0, tiled=True),
        lax.all_gather(down_bias, "fsdp", axis=0, tiled=True),
    )
    gain_two, shift_two, w_up, b_up, w_down, b_down = mlp_set
    gain_two_f = gain_two.astype(jnp.float32)
    shift_two_f = shift_two.astype(jnp.float32)
    normed2 = norm_rows(resid, gain_two_f, shift_two_f).astype(jnp.bfloat16)
    pre = jnp.dot(normed2, w_up, preferred_element_type=jnp.float32) + b_up.astype(jnp.float32)
    hidden = gelu_tanh(pre).astype(jnp.bfloat16)
    result = (
        resid
        + jnp.dot(hidden, w_down, preferred_element_type=jnp.float32)
        + b_down.astype(jnp.float32)
    )
    layer_out = result.astype(jnp.bfloat16)[None]
    cotangent = out_cotangent[0]
    cotangent_f = cotangent.astype(jnp.float32)
    down_w_grad = jnp.einsum("tf,td->fd", hidden, cotangent, preferred_element_type=jnp.float32)
    down_b_grad = jnp.sum(cotangent_f, axis=0)
    hidden_grad = jnp.einsum("td,fd->tf", cotangent, w_down, preferred_element_type=jnp.float32)
    _, gelu_pull = jax.vjp(gelu_tanh, pre)
    pre_grad = gelu_pull(hidden_grad)[0].astype(jnp.bfloat16)
    up_w_grad = jnp.einsum("td,tf->df", normed2, pre_grad, preferred_element_type=jnp.float32)
    up_b_grad = jnp.sum(pre_grad.astype(jnp.float32), axis=0)
    normed2_grad = jnp.einsum("tf,df->td", pre_grad, w_up, preferred_element_type=jnp.float32)
    _, norm_two_pull = jax.vjp(norm_rows, resid, gain_two_f, shift_two_f)
    resid_part, gain_two_grad, shift_two_grad = norm_two_pull(normed2_grad)
    resid_grad = cotangent_f + resid_part
    mlp_sums = (
        lax.psum_scatter(gain_two_grad, ("ctx", "fsdp"), scatter_dimension=0, tiled=True),
        lax.psum_scatter(shift_two_grad, ("ctx", "fsdp"), scatter_dimension=0, tiled=True),
        lax.psum_scatter(up_w_grad, ("ctx", "fsdp"), scatter_dimension=0, tiled=True),
        lax.psum_scatter(up_b_grad, ("ctx", "fsdp"), scatter_dimension=0, tiled=True),
        lax.psum_scatter(down_w_grad, ("ctx", "fsdp"), scatter_dimension=0, tiled=True),
        lax.psum_scatter(down_b_grad, ("ctx", "fsdp"), scatter_dimension=0, tiled=True),
    )
    branch_grad = resid_grad.astype(jnp.bfloat16)
    out_w_grad = jnp.einsum("td,te->de", mix, branch_grad, preferred_element_type=jnp.float32)
    out_b_grad = jnp.sum(branch_grad.astype(jnp.float32), axis=0)
    mix_grad = jnp.einsum(
        "te,de->td", branch_grad, w_out, preferred_element_type=jnp.float32
    ).astype(jnp.bfloat16)
    mix_grad = mix_grad.reshape(tok_rows, HEADS, HEAD_DIM)
    delta = jnp.sum(
        mix_grad.astype(jnp.float32) * mix.reshape(tok_rows, HEADS, HEAD_DIM).astype(jnp.float32),
        axis=2,
    ).T

    def attend_back(query_grad, keys, values, key_grads, value_grads, anchor):
        allowed = block_mask(anchor)
        scores = (
            jnp.einsum("thd,shd->hts", queries, keys, preferred_element_type=jnp.float32)
            * score_scale
        )
        probs = jnp.where(allowed[None], jnp.exp(scores - log_total[:, :, None]), 0.0)
        value_grads = value_grads + jnp.einsum(
            "hts,thd->shd", probs.astype(jnp.bfloat16), mix_grad, preferred_element_type=jnp.float32
        )
        prob_grads = jnp.einsum(
            "thd,shd->hts", mix_grad, values, preferred_element_type=jnp.float32
        )
        score_grads = (probs * (prob_grads - delta[:, :, None])).astype(jnp.bfloat16)
        query_grad = query_grad + score_scale * jnp.einsum(
            "hts,shd->thd", score_grads, keys, preferred_element_type=jnp.float32
        )
        key_grads = key_grads + score_scale * jnp.einsum(
            "hts,thd->shd", score_grads, queries, preferred_element_type=jnp.float32
        )
        return (query_grad, key_grads, value_grads)

    def cycle_backward(cycle_step, state):
        keys, values, key_grads, value_grads, query_grad = state
        anchor = (ctx_index - cycle_step) % ctx_count
        query_grad, key_grads, value_grads = attend_back(
            query_grad, keys, values, key_grads, value_grads, anchor
        )
        keys, values, key_grads, value_grads = (
            from_behind(keys, "ctx", 1),
            from_behind(values, "ctx", 1),
            from_behind(key_grads.astype(jnp.bfloat16), "ctx", 1).astype(key_grads.dtype),
            from_behind(value_grads.astype(jnp.bfloat16), "ctx", 1).astype(value_grads.dtype),
        )
        return (keys, values, key_grads, value_grads, query_grad)

    zero_grads = jnp.zeros((tok_rows, HEADS, HEAD_DIM), jnp.float32)
    back_state = lax.fori_loop(
        0, ctx_count, cycle_backward, (keys_own, values_own, zero_grads, zero_grads, zero_grads)
    )
    key_grads = back_state[2]
    value_grads = back_state[3]
    query_grad = back_state[4]
    qkv_grad = jnp.concatenate(
        [
            query_grad.reshape(tok_rows, model_width),
            key_grads.reshape(tok_rows, model_width),
            value_grads.reshape(tok_rows, model_width),
        ],
        axis=1,
    ).astype(jnp.bfloat16)
    qkv_w_grad = jnp.einsum("td,te->de", normed1, qkv_grad, preferred_element_type=jnp.float32)
    column_sums = jnp.sum(qkv_grad.astype(jnp.float32), axis=0)
    qv_b_grad = jnp.concatenate([column_sums[:model_width], column_sums[2 * model_width :]])
    normed1_grad = jnp.einsum("te,de->td", qkv_grad, w_qkv, preferred_element_type=jnp.float32)
    _, norm_one_pull = jax.vjp(norm_rows, inputs, gain_one_f, shift_one_f)
    input_part, gain_one_grad, shift_one_grad = norm_one_pull(normed1_grad)
    input_grad = (resid_grad + input_part).astype(jnp.bfloat16)[None]
    attn_sums = (
        lax.psum_scatter(gain_one_grad, ("ctx", "fsdp"), scatter_dimension=0, tiled=True),
        lax.psum_scatter(shift_one_grad, ("ctx", "fsdp"), scatter_dimension=0, tiled=True),
        lax.psum_scatter(qkv_w_grad, ("ctx", "fsdp"), scatter_dimension=0, tiled=True),
        lax.psum_scatter(qv_b_grad, ("ctx", "fsdp"), scatter_dimension=0, tiled=True),
        lax.psum_scatter(out_w_grad, ("ctx", "fsdp"), scatter_dimension=0, tiled=True),
        lax.psum_scatter(out_b_grad, ("ctx", "fsdp"), scatter_dimension=0, tiled=True),
    )
    return (
        layer_out,
        input_grad,
        attn_sums[0],
        attn_sums[1],
        attn_sums[2],
        attn_sums[3],
        attn_sums[4],
        attn_sums[5],
        mlp_sums[0],
        mlp_sums[1],
        mlp_sums[2],
        mlp_sums[3],
        mlp_sums[4],
        mlp_sums[5],
    )


def solution(mesh):
    placed = (
        P("fsdp", "ctx", None),
        P("fsdp", None),
        P("fsdp"),
        P("fsdp"),
        P("fsdp", None),
        P("fsdp"),
        P("fsdp", None),
        P("fsdp"),
        P("fsdp"),
        P("fsdp"),
        P("fsdp", None),
        P("fsdp"),
        P("fsdp", None),
        P("fsdp"),
        P("fsdp", "ctx", None),
    )
    return jax.shard_map(
        shards,
        mesh=mesh,
        in_specs=placed,
        out_specs=(
            P("fsdp", "ctx", None),
            P("fsdp", "ctx", None),
            P(("ctx", "fsdp")),
            P(("ctx", "fsdp")),
            P(("ctx", "fsdp"), None),
            P(("ctx", "fsdp")),
            P(("ctx", "fsdp"), None),
            P(("ctx", "fsdp")),
            P(("ctx", "fsdp")),
            P(("ctx", "fsdp")),
            P(("ctx", "fsdp"), None),
            P(("ctx", "fsdp")),
            P(("ctx", "fsdp"), None),
            P(("ctx", "fsdp")),
        ),
        check_vma=False,
    )
```

profile of v0, /device:TPU:0, one launch (start us, length us, event | category | flops | bytes accessed | tf_op | source)
XLA Modules:
  0.0 1537.0 jit_solution(3058902817003224563)
XLA Ops:
  10.2 12.6 all-gather.3
  22.8 13.5 all-gather.2
  36.3 8.5 all-gather.1
  44.8 14.5 all-gather
  60.2 12.0 all_gather.45
  72.2 7.7 all-gather.5
  80.0 13.6 all-gather.4
  93.6 34.6 %all-gather.12.cloned.1.call-done = bf16[1024,3072]{1,0:T(8,128)(2,1)} async-done(((bf16[256,3072]{1,0:T(8,128)(2,1)}), bf16[1024,3072]{1,0:T(8,128)(2,1)}) %all-gather.12.cloned.1.call-update) | async-done | bytes 6291472 | tf_op jit(solution)/shard_map/all_gather | solution.py:74
  136.8 79.3 %while.48 = (s32[]{:T(128)}, bf16[128,16,64]{0,2,1:T(8,128)(2,1)S(1)}, bf16[128,16,64]{0,2,1:T(8,128)(2,1)}, f32[128,16,64]{0,2,1:T(8,128)S(1)}, f32[16,128]{1,0...) while((s32[]{:T(128)}, ...), condition=%wide.region_10.11_spmd.clone, body=%wide.region_6.0_spmd.clone.sunk | while | flops 69264528 | bytes 8294802 | solution.py:124
  144.8 4.9 collective-permute-start
  156.3 4.9 collective-permute-start
  167.8 4.9 collective-permute-start
  179.4 5.2 collective-permute-start
  191.2 5.8 collective-permute-start
  203.7 5.8 collective-permute-start
  218.6 105.3 %all-gather.16.cloned.1.call-done = bf16[1024,4096]{1,0:T(8,128)(2,1)} async-done(((bf16[256,4096]{1,0:T(8,128)(2,1)}), bf16[1024,4096]{1,0:T(8,128)(2,1)}) %all-gather.16.cloned.1.call-update) | async-done | bytes 8388624 | tf_op jit(solution)/shard_map/all_gather | solution.py:136
  323.8 6.1 convolution_add_fusion
  329.9 143.2 %all-gather.18.cloned.1.call-done = bf16[4096,1024]{1,0:T(8,128)(2,1)} async-done(((bf16[1024,1024]{1,0:T(8,128)(2,1)}), bf16[4096,1024]{1,0:T(8,128)(2,1)}) %all-gather.18.cloned.1.call-update) | async-done | bytes 8388624 | tf_op jit(solution)/shard_map/all_gather | solution.py:138
  473.2 7.8 convert_reduce_fusion.2
  490.8 145.1 %while.49 = (s32[]{:T(128)}, bf16[128,16,64]{0,2,1:T(8,128)(2,1)S(1)}, bf16[128,16,64]{0,2,1:T(8,128)(2,1)}, f32[128,16,64]{0,2,1:T(8,128)S(1)}, f32[128,16,64]{...) while((s32[]{:T(128)}, ...), condition=%wide.region_18.19_spmd.clone, body=%wide.region_16.18_spmd.clone.sunk | while | flops 171232400 | bytes 16044550 | solution.py:223
  499.7 4.9 collective-permute-done.4
  536.7 4.7 collective-permute-done.4
  637.1 6.4 fusion.66
  644.8 9.0 fusion.71
  654.8 10.7 fusion.56
  666.2 9.3 all-gather.6
  675.8 5.5 fusion.72
  682.7 43.7 %all-reduce.8 = (f32[1024]{0:T(1024)S(1)}, f32[1024]{0:T(1024)S(1)}, f32[2048]{0:T(1024)S(1)}, f32[1024]{0:T(1024)S(1)}, f32[1024]{0:T(1024)S(1)}, /*index=5*/f3...) all-reduce(f32[1024]{0:T(1024)S(1)} %get-tuple-element.720, ...), channel_id=2, replica_groups=mesh['ctx'=8,'fsdp'=4] {'ctx','fsdp'}, use_global_device_ids=true, to_apply=%region_22.23.clone | all-reduce | flops 12288 | bytes 98304
  731.1 6.5 fusion.37
  737.7 61.1 %reduce-scatter.5.cloned.1.call-done = f32[32,3072]{1,0:T(8,128)} async-done(((f32[1024,3072]{1,0:T(8,128)}), f32[32,3072]{1,0:T(8,128)}) %reduce-scatter.5.cloned.1.call-update) | async-done | bytes 393232 | tf_op jit(solution)/shard_map/reduce_scatter | solution.py:247
  798.7 366.3 %reduce-scatter.9.cloned.1.call-done = f32[32,4096]{1,0:T(8,128)} async-done(((f32[1024,4096]{1,0:T(8,128)}), f32[32,4096]{1,0:T(8,128)}) %reduce-scatter.9.cloned.1.call-update) | async-done | bytes 524304 | tf_op jit(solution)/shard_map/reduce_scatter | solution.py:169
  1165.0 365.1 %reduce-scatter.11.cloned.1.call-done = f32[128,1024]{1,0:T(8,128)} async-done(((f32[4096,1024]{1,0:T(8,128)}), f32[128,1024]{1,0:T(8,128)}) %reduce-scatter.11.cloned.1.call-update) | async-done | bytes 524304 | tf_op jit(solution)/shard_map/reduce_scatter | solution.py:171
  (401 shorter events, 216.4 us)
Async XLA Ops:
  7.2 121.0 %all-gather.12.cloned.1.call-start = ((), (), s32[]{:S(2)}) async-start(), calls=%async_computation.4 | async-start | bytes 7864320 | tf_op jit(solution)/shard_map/all_gather | solution.py:74
  7.9 208.3 %all-gather.14.cloned.1.call-start = ((), (), s32[]{:S(2)}) async-start(), calls=%async_computation.5 | async-start | bytes 2621440 | tf_op jit(solution)/shard_map/all_gather | solution.py:76
  8.8 315.1 %all-gather.16.cloned.1.call-start = ((), (), s32[]{:S(2)}) async-start(), calls=%async_computation.6 | async-start | bytes 10485760 | tf_op jit(solution)/shard_map/all_gather | solution.py:136
  9.5 463.7 %all-gather.18.cloned.1.call-start = ((), (), s32[]{:S(2)}) async-start(), calls=%async_computation.7 | async-start | bytes 10485760 | tf_op jit(solution)/shard_map/all_gather | solution.py:138
  10.1 727.6 %reduce-scatter.7.cloned.1.call-start = ((), (), s32[]{:S(2)}) async-start(), calls=%async_computation.9 | async-start | bytes 4325376 | tf_op jit(solution)/shard_map/reduce_scatter | solution.py:249
  490.8 308.0 %reduce-scatter.5.cloned.1.call-start = ((), (), s32[]{:S(2)}) async-start(), calls=%async_computation.8 | async-start | bytes 12976128 | tf_op jit(solution)/shard_map/reduce_scatter | solution.py:247
  491.1 17.7 %collective-permute-start.2 = (bf16[128,16,64]{0,2,1:T(8,128)(2,1)S(1)}, bf16[128,16,64]{0,2,1:T(8,128)(2,1)S(1)}, u32[]{:S(2)}, u32[]{:S(2)}) collective-permute-start(bf16[128,16,64]{0,2,1:T(8,128)(2,1)S(1)} %copy.89), channel_id=1, source_target_pairs={{0,4},{4,8},{8,12},{12,16},{16,20},{20,24},{24,28},{28,0},{1,5},{5... | collective-permute-start | bytes 786440 | tf_op jit(solution)/shard_map/while/body/eval_jaxpr/ppermute | solution.py:22
  492.1 16.6 %collective-permute-start.3 = (bf16[128,16,64]{0,2,1:T(8,128)(2,1)S(1)}, bf16[128,16,64]{0,2,1:T(8,128)(2,1)}, u32[]{:S(2)}, u32[]{:S(2)}) collective-permute-start(bf16[128,16,64]{0,2,1:T(8,128)(2,1)S(1)} %copy.90), channel_id=1, source_target_pairs={{0,4},{4,8},{8,12},{12,16},{16,20},{20,24},{24,28},{28,0},{1,5},{5... | collective-permute-start | bytes 786440 | tf_op jit(solution)/shard_map/while/body/eval_jaxpr/ppermute | solution.py:22
  508.8 18.3 %collective-permute-start.2 = (bf16[128,16,64]{0,2,1:T(8,128)(2,1)S(1)}, bf16[128,16,64]{0,2,1:T(8,128)(2,1)S(1)}, u32[]{:S(2)}, u32[]{:S(2)}) collective-permute-start(bf16[128,16,64]{0,2,1:T(8,128)(2,1)S(1)} %copy.89), channel_id=1, source_target_pairs={{0,4},{4,8},{8,12},{12,16},{16,20},{20,24},{24,28},{28,0},{1,5},{5... | collective-permute-start | bytes 786440 | tf_op jit(solution)/shard_map/while/body/eval_jaxpr/ppermute | solution.py:22
  509.8 17.3 %collective-permute-start.3 = (bf16[128,16,64]{0,2,1:T(8,128)(2,1)S(1)}, bf16[128,16,64]{0,2,1:T(8,128)(2,1)}, u32[]{:S(2)}, u32[]{:S(2)}) collective-permute-start(bf16[128,16,64]{0,2,1:T(8,128)(2,1)S(1)} %copy.90), channel_id=1, source_target_pairs={{0,4},{4,8},{8,12},{12,16},{16,20},{20,24},{24,28},{28,0},{1,5},{5... | collective-permute-start | bytes 786440 | tf_op jit(solution)/shard_map/while/body/eval_jaxpr/ppermute | solution.py:22
  513.7 12.4 collective-permute-start.5
  527.2 18.2 %collective-permute-start.2 = (bf16[128,16,64]{0,2,1:T(8,128)(2,1)S(1)}, bf16[128,16,64]{0,2,1:T(8,128)(2,1)S(1)}, u32[]{:S(2)}, u32[]{:S(2)}) collective-permute-start(bf16[128,16,64]{0,2,1:T(8,128)(2,1)S(1)} %copy.89), channel_id=1, source_target_pairs={{0,4},{4,8},{8,12},{12,16},{16,20},{20,24},{24,28},{28,0},{1,5},{5... | collective-permute-start | bytes 786440 | tf_op jit(solution)/shard_map/while/body/eval_jaxpr/ppermute | solution.py:22
  528.2 17.2 %collective-permute-start.3 = (bf16[128,16,64]{0,2,1:T(8,128)(2,1)S(1)}, bf16[128,16,64]{0,2,1:T(8,128)(2,1)}, u32[]{:S(2)}, u32[]{:S(2)}) collective-permute-start(bf16[128,16,64]{0,2,1:T(8,128)(2,1)S(1)} %copy.90), channel_id=1, source_target_pairs={{0,4},{4,8},{8,12},{12,16},{16,20},{20,24},{24,28},{28,0},{1,5},{5... | collective-permute-start | bytes 786440 | tf_op jit(solution)/shard_map/while/body/eval_jaxpr/ppermute | solution.py:22
  530.4 11.0 collective-permute-start.4
  531.4 13.0 collective-permute-start.5
  545.4 18.1 %collective-permute-start.2 = (bf16[128,16,64]{0,2,1:T(8,128)(2,1)S(1)}, bf16[128,16,64]{0,2,1:T(8,128)(2,1)S(1)}, u32[]{:S(2)}, u32[]{:S(2)}) collective-permute-start(bf16[128,16,64]{0,2,1:T(8,128)(2,1)S(1)} %copy.89), channel_id=1, source_target_pairs={{0,4},{4,8},{8,12},{12,16},{16,20},{20,24},{24,28},{28,0},{1,5},{5... | collective-permute-start | bytes 786440 | tf_op jit(solution)/shard_map/while/body/eval_jaxpr/ppermute | solution.py:22
  546.5 17.1 %collective-permute-start.3 = (bf16[128,16,64]{0,2,1:T(8,128)(2,1)S(1)}, bf16[128,16,64]{0,2,1:T(8,128)(2,1)}, u32[]{:S(2)}, u32[]{:S(2)}) collective-permute-start(bf16[128,16,64]{0,2,1:T(8,128)(2,1)S(1)} %copy.90), channel_id=1, source_target_pairs={{0,4},{4,8},{8,12},{12,16},{16,20},{20,24},{24,28},{28,0},{1,5},{5... | collective-permute-start | bytes 786440 | tf_op jit(solution)/shard_map/while/body/eval_jaxpr/ppermute | solution.py:22
  549.7 12.8 collective-permute-start.5
  563.6 18.0 %collective-permute-start.2 = (bf16[128,16,64]{0,2,1:T(8,128)(2,1)S(1)}, bf16[128,16,64]{0,2,1:T(8,128)(2,1)S(1)}, u32[]{:S(2)}, u32[]{:S(2)}) collective-permute-start(bf16[128,16,64]{0,2,1:T(8,128)(2,1)S(1)} %copy.89), channel_id=1, source_target_pairs={{0,4},{4,8},{8,12},{12,16},{16,20},{20,24},{24,28},{28,0},{1,5},{5... | collective-permute-start | bytes 786440 | tf_op jit(solution)/shard_map/while/body/eval_jaxpr/ppermute | solution.py:22
  564.6 17.0 %collective-permute-start.3 = (bf16[128,16,64]{0,2,1:T(8,128)(2,1)S(1)}, bf16[128,16,64]{0,2,1:T(8,128)(2,1)}, u32[]{:S(2)}, u32[]{:S(2)}) collective-permute-start(bf16[128,16,64]{0,2,1:T(8,128)(2,1)S(1)} %copy.90), channel_id=1, source_target_pairs={{0,4},{4,8},{8,12},{12,16},{16,20},{20,24},{24,28},{28,0},{1,5},{5... | collective-permute-start | bytes 786440 | tf_op jit(solution)/shard_map/while/body/eval_jaxpr/ppermute | solution.py:22
  567.8 12.8 collective-permute-start.5
  581.7 18.0 %collective-permute-start.2 = (bf16[128,16,64]{0,2,1:T(8,128)(2,1)S(1)}, bf16[128,16,64]{0,2,1:T(8,128)(2,1)S(1)}, u32[]{:S(2)}, u32[]{:S(2)}) collective-permute-start(bf16[128,16,64]{0,2,1:T(8,128)(2,1)S(1)} %copy.89), channel_id=1, source_target_pairs={{0,4},{4,8},{8,12},{12,16},{16,20},{20,24},{24,28},{28,0},{1,5},{5... | collective-permute-start | bytes 786440 | tf_op jit(solution)/shard_map/while/body/eval_jaxpr/ppermute | solution.py:22
  582.7 17.0 %collective-permute-start.3 = (bf16[128,16,64]{0,2,1:T(8,128)(2,1)S(1)}, bf16[128,16,64]{0,2,1:T(8,128)(2,1)}, u32[]{:S(2)}, u32[]{:S(2)}) collective-permute-start(bf16[128,16,64]{0,2,1:T(8,128)(2,1)S(1)} %copy.90), channel_id=1, source_target_pairs={{0,4},{4,8},{8,12},{12,16},{16,20},{20,24},{24,28},{28,0},{1,5},{5... | collective-permute-start | bytes 786440 | tf_op jit(solution)/shard_map/while/body/eval_jaxpr/ppermute | solution.py:22
  586.0 12.7 collective-permute-start.5
  599.8 18.0 %collective-permute-start.2 = (bf16[128,16,64]{0,2,1:T(8,128)(2,1)S(1)}, bf16[128,16,64]{0,2,1:T(8,128)(2,1)S(1)}, u32[]{:S(2)}, u32[]{:S(2)}) collective-permute-start(bf16[128,16,64]{0,2,1:T(8,128)(2,1)S(1)} %copy.89), channel_id=1, source_target_pairs={{0,4},{4,8},{8,12},{12,16},{16,20},{20,24},{24,28},{28,0},{1,5},{5... | collective-permute-start | bytes 786440 | tf_op jit(solution)/shard_map/while/body/eval_jaxpr/ppermute | solution.py:22
  600.8 17.0 %collective-permute-start.3 = (bf16[128,16,64]{0,2,1:T(8,128)(2,1)S(1)}, bf16[128,16,64]{0,2,1:T(8,128)(2,1)}, u32[]{:S(2)}, u32[]{:S(2)}) collective-permute-start(bf16[128,16,64]{0,2,1:T(8,128)(2,1)S(1)} %copy.90), channel_id=1, source_target_pairs={{0,4},{4,8},{8,12},{12,16},{16,20},{20,24},{24,28},{28,0},{1,5},{5... | collective-permute-start | bytes 786440 | tf_op jit(solution)/shard_map/while/body/eval_jaxpr/ppermute | solution.py:22
  604.5 12.3 collective-permute-start.5
  617.9 18.0 %collective-permute-start.2 = (bf16[128,16,64]{0,2,1:T(8,128)(2,1)S(1)}, bf16[128,16,64]{0,2,1:T(8,128)(2,1)S(1)}, u32[]{:S(2)}, u32[]{:S(2)}) collective-permute-start(bf16[128,16,64]{0,2,1:T(8,128)(2,1)S(1)} %copy.89), channel_id=1, source_target_pairs={{0,4},{4,8},{8,12},{12,16},{16,20},{20,24},{24,28},{28,0},{1,5},{5... | collective-permute-start | bytes 786440 | tf_op jit(solution)/shard_map/while/body/eval_jaxpr/ppermute | solution.py:22
  618.9 17.0 %collective-permute-start.3 = (bf16[128,16,64]{0,2,1:T(8,128)(2,1)S(1)}, bf16[128,16,64]{0,2,1:T(8,128)(2,1)}, u32[]{:S(2)}, u32[]{:S(2)}) collective-permute-start(bf16[128,16,64]{0,2,1:T(8,128)(2,1)S(1)} %copy.90), channel_id=1, source_target_pairs={{0,4},{4,8},{8,12},{12,16},{16,20},{20,24},{24,28},{28,0},{1,5},{5... | collective-permute-start | bytes 786440 | tf_op jit(solution)/shard_map/while/body/eval_jaxpr/ppermute | solution.py:22
  623.0 11.9 collective-permute-start.5
  643.6 521.4 %reduce-scatter.9.cloned.1.call-start = ((), (), s32[]{:S(2)}) async-start(), calls=%async_computation.10 | async-start | bytes 17301504 | tf_op jit(solution)/shard_map/reduce_scatter | solution.py:169
  653.8 876.3 %reduce-scatter.11.cloned.1.call-start = ((), (), s32[]{:S(2)}) async-start(), calls=%async_computation.11 | async-start | bytes 17301504 | tf_op jit(solution)/shard_map/reduce_scatter | solution.py:171
  (40 other events, 724.4 us)
Sparse Core Ops, SparseCore 0:
  9.6 118.5 all-gather.11
  129.7 44.0 all-gather.13
  175.5 148.3 all-gather.15
  325.3 147.8 all-gather.17
  490.9 145.9 reduce-scatter.6
  643.7 154.9 reduce-scatter.4
  801.7 363.2 reduce-scatter.8
  1168.0 362.1 reduce-scatter.10
where the time goes:
time: 1540 us
  waiting for transfers between devices  1130 us (73%)
  blocking collectives  135 us (9%)
  matrix products  114 us (7%)
  starting transfers between devices  90.4 us (6%)
  other arithmetic  24.6 us (2%)
  local copies, waits for them, and re-layouts  24.2 us (2%)
    reduce_scatter x1, waiting for transfers between devices, shards(): lax.psum_scatter(up_w_grad, ('ctx', 'fsdp'), scatter_dimension=0, tiled=T...  366 us
    reduce_scatter x1, waiting for transfers between devices, shards(): lax.psum_scatter(down_w_grad, ('ctx', 'fsdp'), scatter_dimension=0, tiled...  365 us
    all_gather x1, waiting for transfers between devices, shards(): lax.all_gather(down_weight, 'fsdp', axis=0, tiled=True)  143 us
    all_gather x1, waiting for transfers between devices, shards(): lax.all_gather(up_weight, 'fsdp', axis=0, tiled=True)  105 us
    ppermute x14, starting transfers between devices, passed_along(): return lax.ppermute(block, axis, route)  62.4 us
    reduce_scatter x1, waiting for transfers between devices, shards(): lax.psum_scatter(qkv_w_grad, ('ctx', 'fsdp'), scatter_dimension=0, tiled=...  61.1 us
    ppermute x32, waiting for transfers between devices, from_behind(): return lax.ppermute(x, axis, [(i, (i + by) % size) for i in range(size)])  50 us
    unnamed x1, blocking collectives  43.7 us
  transfers between devices with their start and end apart: 54, of which 29 were waited for; matrix products, arithmetic and copies ran while one was open for 9% of the time, Pallas kernels for 0%

commit v1 on v0

v1 whole, which is shorter than its diff:
```python
import jax
import jax.numpy as jnp
from jax import lax
from jax.sharding import PartitionSpec as P

HEADS = 16
HEAD_DIM = 64

epsilon = 1e-05
masked_score = -1e30
f32 = jnp.float32
bf16 = jnp.bfloat16


def row_stats(values):
    mean = jnp.mean(values, axis=-1, keepdims=True)
    centre = values - mean
    spread = jnp.mean(centre * centre, axis=-1, keepdims=True)
    scale = lax.rsqrt(spread + epsilon)
    return centre * scale, scale


def norm_back(grad, xhat, scale, gain):
    gh = grad * gain
    return scale * (
        gh
        - jnp.mean(gh, axis=-1, keepdims=True)
        - xhat * jnp.mean(gh * xhat, axis=-1, keepdims=True)
    )


def gelu_both(v):
    k = 0.7978845608028654
    inner = jnp.tanh(k * (v + 0.044715 * v * v * v))
    value = 0.5 * v * (1.0 + inner)
    slope = 0.5 * (1.0 + inner) + 0.5 * v * (1.0 - inner * inner) * k * (
        1.0 + 3 * 0.044715 * v * v
    )
    return value, slope


def mm(a, b, dims):
    return lax.dot_general(a, b, (dims, ((), ())), preferred_element_type=f32)


NN = ((1,), (0,))
NT = ((1,), (1,))
TN = ((0,), (0,))


def columns(weight, start, width):
    return lax.dynamic_slice_in_dim(weight, start, width, axis=1)


def shards(
    tokens_in,
    doc_lengths,
    norm1_gain,
    norm1_bias,
    qkv_weight,
    qv_bias,
    out_weight,
    out_bias,
    norm2_gain,
    norm2_bias,
    up_weight,
    up_bias,
    down_weight,
    down_bias,
    out_cotangent,
):
    C = lax.axis_size("ctx")
    Z = lax.axis_size("fsdp")
    c = lax.axis_index("ctx")
    rows, width = tokens_in.shape[1:]
    seq = rows * C
    heads = HEADS // C
    hw = heads * HEAD_DIM
    ff = up_weight.shape[1]
    fw = ff // C
    score_scale = HEAD_DIM ** (-0.5)

    def along_z(x):
        return lax.all_gather(x, "fsdp", axis=0, tiled=True)

    def along_ctx(x):
        return lax.all_gather(x, "ctx", axis=0, tiled=True)

    def scatter_ctx(x):
        return lax.psum_scatter(x.astype(bf16), "ctx", scatter_dimension=0, tiled=True).astype(f32)

    vectors = jnp.concatenate(
        [norm1_gain, norm1_bias, qv_bias, out_bias, norm2_gain, norm2_bias, up_bias, down_bias]
    )
    vectors = lax.all_gather(vectors, "fsdp", axis=0)
    sizes = [
        v.shape[0]
        for v in (norm1_gain, norm1_bias, qv_bias, out_bias, norm2_gain, norm2_bias, up_bias, down_bias)
    ]
    pieces, at = [], 0
    for size in sizes:
        pieces.append(vectors[:, at : at + size].reshape(-1).astype(f32))
        at += size
    gain_one, shift_one, b_qv, b_out, gain_two, shift_two, b_up, b_down = pieces

    w_qkv_part = jnp.concatenate(
        [columns(qkv_weight, part * width + c * hw, hw) for part in range(3)], axis=1
    )
    w_qkv = along_z(w_qkv_part)
    out_rows = width // C
    w_out_full = along_z(out_weight)
    w_out = lax.dynamic_slice_in_dim(w_out_full, c * out_rows, out_rows, axis=0)
    w_up = along_z(columns(up_weight, c * fw, fw))
    w_down_full = along_z(down_weight)
    w_down = lax.dynamic_slice_in_dim(w_down_full, c * fw, fw, axis=0)

    x = tokens_in[0].astype(f32)
    xhat1, scale1 = row_stats(x)
    n1 = along_ctx((xhat1 * gain_one + shift_one).astype(bf16))
    bias_q = lax.dynamic_slice_in_dim(b_qv, c * hw, hw)
    bias_v = lax.dynamic_slice_in_dim(b_qv, width + c * hw, hw)
    qkv = mm(n1, w_qkv, NN) + jnp.concatenate([bias_q, jnp.zeros((hw,), f32), bias_v])
    qkv = qkv.astype(bf16)

    ends = jnp.cumsum(doc_lengths[0])
    pos = jnp.arange(seq, dtype=jnp.int32)
    doc = jnp.sum((ends[None, :] <= pos[:, None]).astype(jnp.int32), axis=1)
    allowed = (pos[None, :] <= pos[:, None]) & (doc[None, :] == doc[:, None])

    def head(part, h):
        at = part * hw + h * HEAD_DIM
        return qkv[:, at : at + HEAD_DIM]

    mixes, lses = [], []
    for h in range(heads):
        s = mm(head(0, h), head(1, h), NT) * score_scale
        s = jnp.where(allowed, s, masked_score)
        top = jnp.max(s, axis=1, keepdims=True)
        e = jnp.exp(s - top)
        total = jnp.sum(e, axis=1, keepdims=True)
        mixes.append((mm(e.astype(bf16), head(2, h), NN) / total).astype(bf16))
        lses.append(top + jnp.log(total))
    mix = jnp.concatenate(mixes, axis=1)

    resid = x + scatter_ctx(mm(mix, w_out, NN)) + b_out
    xhat2, scale2 = row_stats(resid)
    n2 = along_ctx((xhat2 * gain_two + shift_two).astype(bf16))
    pre = mm(n2, w_up, NN) + lax.dynamic_slice_in_dim(b_up, c * fw, fw)
    value, slope = gelu_both(pre)
    hidden = value.astype(bf16)
    layer_out = (resid + scatter_ctx(mm(hidden, w_down, NN)) + b_down).astype(bf16)[None]

    cot = along_ctx(out_cotangent[0])
    hidden_grad = mm(cot, w_down, NT)
    pre_grad = (hidden_grad * slope).astype(bf16)
    down_w_grad = mm(hidden, cot, TN)
    up_w_grad = mm(n2, pre_grad, TN)
    up_b_grad = jnp.sum(pre_grad.astype(f32), axis=0)
    n2_grad = scatter_ctx(mm(pre_grad, w_up, NT))
    cot_own = out_cotangent[0].astype(f32)
    resid_grad = cot_own + norm_back(n2_grad, xhat2, scale2, gain_two)
    branch_own = resid_grad.astype(bf16)
    branch = along_ctx(branch_own)
    out_w_grad = mm(mix, branch, TN)
    mix_grad = mm(branch, w_out, NT).astype(bf16)

    grads = [[], [], []]
    for h in range(heads):
        at = h * HEAD_DIM
        q, k, v = (head(part, h) for part in range(3))
        g = mix_grad[:, at : at + HEAD_DIM]
        p = jnp.where(allowed, jnp.exp(mm(q, k, NT) * score_scale - lses[h]), 0.0)
        delta = jnp.sum(g.astype(f32) * mixes[h].astype(f32), axis=1, keepdims=True)
        ds = (p * (mm(g, v, NT) - delta)).astype(bf16)
        grads[0].append(score_scale * mm(ds, k, NN))
        grads[1].append(score_scale * mm(ds, q, TN))
        grads[2].append(mm(p.astype(bf16), g, TN))
    qkv_grad = jnp.concatenate(grads[0] + grads[1] + grads[2], axis=1).astype(bf16)

    qkv_w_grad = mm(n1, qkv_grad, TN)
    qkv_sums = jnp.sum(qkv_grad.astype(f32), axis=0)
    n1_grad = scatter_ctx(mm(qkv_grad, w_qkv, NT))
    input_grad = (resid_grad + norm_back(n1_grad, xhat1, scale1, gain_one)).astype(bf16)[None]

    def rows_home(grad):
        return lax.psum_scatter(grad.astype(bf16), "fsdp", scatter_dimension=0, tiled=True).astype(f32)

    def columns_home(grad):
        r = grad.shape[0] // (C * Z)
        grad = grad.astype(bf16).reshape(C, Z, r, grad.shape[1])
        mine = lax.psum_scatter(grad, "fsdp", scatter_dimension=1, tiled=True)[:, 0]
        return lax.all_to_all(mine, "ctx", 0, 0, tiled=False).astype(f32)

    d_down = rows_home(down_w_grad)
    d_out = rows_home(out_w_grad)
    up_parts = columns_home(up_w_grad)
    d_up = up_parts.transpose(1, 0, 2).reshape(-1, ff)
    qkv_parts = columns_home(qkv_w_grad)
    r = qkv_parts.shape[1]
    d_qkv = qkv_parts.reshape(C, r, 3, hw).transpose(1, 2, 0, 3).reshape(r, 3 * width)

    def spread(v, size):
        return lax.dynamic_update_slice(jnp.zeros((size,), f32), v, (c * v.shape[0],))

    parts = [
        jnp.sum(n1_grad * xhat1, axis=0),
        jnp.sum(n1_grad, axis=0),
        jnp.concatenate([spread(qkv_sums[:hw], width), spread(qkv_sums[2 * hw :], width)]),
        jnp.sum(branch_own.astype(f32), axis=0),
        jnp.sum(n2_grad * xhat2, axis=0),
        jnp.sum(n2_grad, axis=0),
        spread(up_b_grad, ff),
        jnp.sum(cot_own, axis=0),
    ]
    packed = jnp.concatenate([p.reshape(C * Z, -1) for p in parts], axis=1)
    packed = lax.psum_scatter(packed, ("ctx", "fsdp"), scatter_dimension=0, tiled=True)[0]
    small, at = [], 0
    for p in parts:
        n = p.shape[0] // (C * Z)
        small.append(packed[at : at + n])
        at += n
    return (
        layer_out,
        input_grad,
        small[0],
        small[1],
        d_qkv,
        small[2],
        d_out,
        small[3],
        small[4],
        small[5],
        d_up,
        small[6],
        d_down,
        small[7],
    )


def solution(mesh):
    token = P("fsdp", "ctx", None)
    flat, table = P("fsdp"), P("fsdp", None)
    home, home2 = P(("ctx", "fsdp")), P(("ctx", "fsdp"), None)
    return jax.shard_map(
        shards,
        mesh=mesh,
        in_specs=(
            token, table, flat, flat, table, flat, table, flat,
            flat, flat, table, flat, table, flat, token,
        ),
        out_specs=(
            token, token, home, home, home2, home, home2, home,
            home, home, home2, home, home2, home,
        ),
        check_vma=False,
    )
```

time: 1540 us -> 744 us (0.48)
  waiting for transfers between devices: 1130 us -> 542 us
  starting transfers between devices: 90.4 us -> 8.69 us
  blocking collectives: 135 us -> 72.1 us
  matrix products: 114 us -> 57 us
    reduce_scatter x4 -> x7, waiting for transfers between devices: 793 us -> 214 us  [the longest x4 155 us: scatter_ctx(): lax.psum_scatter(x.astype(bf16), 'ctx', scatter_dimension=0, tiled=True)]
    ppermute x46 -> x0, starting transfers between devices: 90 us -> none  [the longest x14 62.4 us: passed_along(): return lax.ppermute(block, axis, route)]
    all_gather x8 -> x2, blocking collectives: 91.7 us -> 32.4 us  [the longest x1 17.6 us: along_z(): return lax.all_gather(x, 'fsdp', axis=0, tiled=True)]
    dot_general x68 -> x24, matrix products: 114 us -> 57 us  [mm(): return lax.dot_general(a, b, (dims, ((), ())), preferred_element_type=f32)]
    ppermute x46 -> x0, waiting for transfers between devices: 53.4 us -> none  [the longest x32 50 us: from_behind(): return lax.ppermute(x, axis, [(i, (i + by) % size) for i in range(size)])]
    unnamed x8 -> x16, waiting for transfers between devices: 2.65 us -> 31.6 us
    all_gather x4 -> x7, waiting for transfers between devices: 283 us -> 297 us  [the longest x3 214 us: along_z(): return lax.all_gather(x, 'fsdp', axis=0, tiled=True)]
  transfers between devices with their start and end apart: 54 -> 17, of which waited for: 29 -> 15; matrix products, arithmetic and copies ran while one was open for 9% -> 10% of each run, Pallas kernels for 0% -> 0%
where the time goes in v1:
time: 744 us; the launch traced here: 742 us
  waiting for transfers between devices  542 us (73%)
  blocking collectives  72.1 us (10%)
  matrix products  57 us (8%)
  other arithmetic  24.9 us (3%)
  local copies, waits for them, and re-layouts  22.9 us (3%)
  between operations  14.6 us (2%)
  starting transfers between devices  8.69 us (1%)
    all_gather x3, waiting for transfers between devices, along_z(): return lax.all_gather(x, 'fsdp', axis=0, tiled=True)  214 us
    reduce_scatter x4, waiting for transfers between devices, scatter_ctx(): lax.psum_scatter(x.astype(bf16), 'ctx', scatter_dimension=0, tiled=True)  155 us
    all_gather x4, waiting for transfers between devices, along_ctx(): return lax.all_gather(x, 'ctx', axis=0, tiled=True)  82.7 us
    dot_general x24, matrix products, mm(): return lax.dot_general(a, b, (dims, ((), ())), preferred_element_type=f32)  57 us
    unnamed x1, blocking collectives  39.8 us
    reduce_scatter x2, waiting for transfers between devices, rows_home(): lax.psum_scatter(grad.astype(bf16), 'fsdp', scatter_dimension=0, tiled=True)  39.2 us
    unnamed x16, waiting for transfers between devices  31.6 us
    reduce_scatter x1, waiting for transfers between devices, columns_home(): mine = lax.psum_scatter(grad, 'fsdp', scatter_dimension=1, tiled=True)[:, 0]  20 us
  transfers between devices with their start and end apart: 17, of which 15 were waited for; matrix products, arithmetic and copies ran while one was open for 10% of the time, Pallas kernels for 0%

profile of v1, /device:TPU:0, one launch (start us, length us, event | category | flops | bytes accessed | tf_op | source)
XLA Modules:
  0.0 742.4 jit_solution(18043129602330694830)
XLA Ops:
  16.4 14.8 %all-gather = bf16[12288]{0:T(1024)(128)(2,1)S(1)} all-gather(bf16[3072]{0:T(1024)(128)(2,1)S(1)} %dynamic-update-slice.13), channel_id=2, replica_groups=mesh['ctx'=8,'fsdp'=4] {'fsdp'}, dimensions={0}, use_global_device_ids=true | all-gather | bytes 30720 | tf_op jit(solution)/shard_map/all_gather | solution.py:95
  36.0 17.6 %all_gather.33 = bf16[1024,384]{1,0:T(8,128)(2,1)S(1)} all-gather(bf16[256,384]{1,0:T(8,128)(2,1)S(1)} %pad_maximum_fusion.1), channel_id=1, replica_groups=mesh['ctx'=8,'fsdp'=4] {'fsdp'}, dimensions={0}, use_global_device_ids=true | all-gather | bytes 983040 | tf_op jit(solution)/shard_map/all_gather | solution.py:84
  53.6 8.7 %all-gather.10.cloned.1.call-done = bf16[1024,1024]{1,0:T(8,128)(2,1)} async-done(((bf16[128,1024]{1,0:T(8,128)(2,1)}), bf16[1024,1024]{1,0:T(8,128)(2,1)}) %all-gather.10.cloned.1.call-update) | async-done | bytes 2097168 | tf_op jit(solution)/shard_map/all_gather | solution.py:87
  62.3 2.6 add_convert_fusion
  71.3 38.5 %all-gather.12.cloned.1.call-done = bf16[1024,1024]{1,0:T(8,128)(2,1)} async-done(((bf16[256,1024]{1,0:T(8,128)(2,1)}), bf16[1024,1024]{1,0:T(8,128)(2,1)}) %all-gather.12.cloned.1.call-update) | async-done | bytes 2097168 | tf_op jit(solution)/shard_map/all_gather | solution.py:84
  109.8 3.0 convolution_convert_fusion.3
  113.7 39.3 %reduce-scatter.11.cloned.1.call-done = bf16[128,1024]{1,0:T(8,128)(2,1)} async-done(((bf16[1024,1024]{1,0:T(8,128)(2,1)}), bf16[128,1024]{1,0:T(8,128)(2,1)}) %reduce-scatter.11.cloned.1.call-update) | async-done | bytes 262160 | tf_op jit(solution)/shard_map/reduce_scatter | solution.py:90
  158.9 24.2 %all-gather.16.cloned.1.call-done = bf16[1024,512]{1,0:T(8,128)(2,1)} async-done(((bf16[256,512]{1,0:T(8,128)(2,1)}), bf16[1024,512]{1,0:T(8,128)(2,1)}) %all-gather.16.cloned.1.call-update) | async-done | bytes 1048592 | tf_op jit(solution)/shard_map/all_gather | solution.py:84
  183.1 29.9 %all-gather.14.cloned.1.call-done = bf16[1024,1024]{1,0:T(8,128)(2,1)} async-done(((bf16[128,1024]{1,0:T(8,128)(2,1)}), bf16[1024,1024]{1,0:T(8,128)(2,1)}) %all-gather.14.cloned.1.call-update) | async-done | bytes 2097168 | tf_op jit(solution)/shard_map/all_gather | solution.py:87
  213.0 4.5 fusion.137
  217.4 25.4 %all-gather.22.cloned.1.call-done = bf16[1,1024,1024]{2,1,0:T(8,128)(2,1)} async-done(((bf16[1,128,1024]{2,1,0:T(8,128)(2,1)}), bf16[1,1024,1024]{2,1,0:T(8,128)(2,1)}) %all-gather.22.cloned.1.call-update) | async-done | bytes 2097168 | tf_op jit(solution)/shard_map/all_gather | solution.py:87
  242.8 151.3 %all-gather.18.cloned.1.call-done = bf16[4096,1024]{1,0:T(8,128)(2,1)} async-done(((bf16[1024,1024]{1,0:T(8,128)(2,1)}), bf16[4096,1024]{1,0:T(8,128)(2,1)}) %all-gather.18.cloned.1.call-update) | async-done | bytes 8388624 | tf_op jit(solution)/shard_map/all_gather | solution.py:84
  394.1 5.6 convert_reduce_fusion
  400.7 2.6 convolution_convert_fusion.1
  403.4 4.7 convolution_convert_fusion.2
  408.7 34.2 %reduce-scatter.15.cloned.1.call-done = bf16[128,1024]{1,0:T(8,128)(2,1)} async-done(((bf16[1024,1024]{1,0:T(8,128)(2,1)}), bf16[128,1024]{1,0:T(8,128)(2,1)}) %reduce-scatter.15.cloned.1.call-update) | async-done | bytes 262160 | tf_op jit(solution)/shard_map/reduce_scatter | solution.py:90
  445.4 42.1 %reduce-scatter.13.cloned.1.call-done = bf16[128,1024]{1,0:T(8,128)(2,1)} async-done(((bf16[1024,1024]{1,0:T(8,128)(2,1)}), bf16[128,1024]{1,0:T(8,128)(2,1)}) %reduce-scatter.13.cloned.1.call-update) | async-done | bytes 262160 | tf_op jit(solution)/shard_map/reduce_scatter | solution.py:90
  487.5 2.8 convert_reduce_fusion.6
  490.4 4.1 convolution_convert_fusion.4
  494.7 4.6 fusion.32
  499.6 18.8 %all-gather.20.cloned.1.call-done = bf16[1024,1024]{1,0:T(8,128)(2,1)} async-done(((bf16[128,1024]{1,0:T(8,128)(2,1)}), bf16[1024,1024]{1,0:T(8,128)(2,1)}) %all-gather.20.cloned.1.call-update) | async-done | bytes 2097168 | tf_op jit(solution)/shard_map/all_gather | solution.py:87
  521.0 3.8 multiply_convert_fusion
  535.7 2.7 convolution_convert_fusion.6
  538.5 4.0 convolution_convert_fusion
  543.2 29.5 %all-reduce.4.cloned.1.call-done = bf16[8,4,32,512]{3,2,1,0:T(8,128)(2,1)} async-done(((bf16[8,4,32,512]{3,2,1,0:T(8,128)(2,1)}), bf16[8,4,32,512]{3,2,1,0:T(8,128)(2,1)}) %all-reduce.4.cloned.1.call-update) | async-done | bytes 1048592
  575.0 3.7 all-to-all-start.1
  579.1 22.4 %reduce-scatter.23.cloned.1.call-done = bf16[128,1024]{1,0:T(8,128)(2,1)} async-done(((bf16[512,1024]{1,0:T(8,128)(2,1)}), bf16[128,1024]{1,0:T(8,128)(2,1)}) %reduce-scatter.23.cloned.1.call-update) | async-done | bytes 262160 | tf_op jit(solution)/shard_map/reduce_scatter | solution.py:186
  605.8 20.0 %reduce-scatter.19.cloned.1.call-done = bf16[8,1,32,384]{3,2,0,1:T(8,128)(2,1)} async-done(((bf16[8,4,32,384]{3,2,0,1:T(8,128)(2,1)}), bf16[8,1,32,384]{3,2,0,1:T(8,128)(2,1)}) %reduce-scatter.19.cloned.1.call-update) | async-done | bytes 196624 | tf_op jit(solution)/shard_map/reduce_scatter | solution.py:191
  625.8 4.0 all-to-all-start
  630.7 16.8 %reduce-scatter.21.cloned.1.call-done = bf16[32,1024]{1,0:T(8,128)(2,1)} async-done(((bf16[128,1024]{1,0:T(8,128)(2,1)}), bf16[32,1024]{1,0:T(8,128)(2,1)}) %reduce-scatter.21.cloned.1.call-update) | async-done | bytes 65552 | tf_op jit(solution)/shard_map/reduce_scatter | solution.py:186
  651.2 39.0 %reduce-scatter.17.cloned.1.call-done = bf16[128,1024]{1,0:T(8,128)(2,1)} async-done(((bf16[1024,1024]{1,0:T(8,128)(2,1)}), bf16[128,1024]{1,0:T(8,128)(2,1)}) %reduce-scatter.17.cloned.1.call-update) | async-done | bytes 262160 | tf_op jit(solution)/shard_map/reduce_scatter | solution.py:90
  692.4 39.8 %all-reduce = f32[32,384]{1,0:T(8,128)S(1)} all-reduce(f32[32,384]{1,0:T(8,128)S(1)} %concatenate.35), channel_id=8, replica_groups=mesh['ctx'=8,'fsdp'=4] {'ctx','fsdp'}, use_global_device_ids=true, to_apply=%region_28.29.clone | all-reduce | flops 12288 | bytes 98304
  (203 shorter events, 62.8 us)
Async XLA Ops:
  7.2 105.7 %copy-start = (bf16[256,4096]{1,0:T(8,128)(2,1)S(1)}, bf16[256,4096]{1,0:T(8,128)(2,1)}, u32[]{:S(2)}) copy-start(bf16[256,4096]{1,0:T(8,128)(2,1)} %param.25) | copy-start | bytes 6291460
  7.2 55.1 %all-gather.10.cloned.1.call-start = ((), (), s32[]{:S(2)}) async-start(), calls=%async_computation.9 | async-start | bytes 2359296 | tf_op jit(solution)/shard_map/all_gather | solution.py:87
  9.6 55.2 %copy-start.23 = (f32[128]{0:T(128)}, f32[128]{0:T(128)S(1)}, u32[]{:S(2)}) copy-start(f32[128]{0:T(128)S(1)} %add_rsqrt_fusion.1) | copy-start | bytes 1540
  33.1 76.6 %all-gather.12.cloned.1.call-start = ((), (), s32[]{:S(2)}) async-start(), calls=%async_computation.10 | async-start | bytes 2621440 | tf_op jit(solution)/shard_map/all_gather | solution.py:84
  33.9 119.2 %reduce-scatter.11.cloned.1.call-start = ((), (), s32[]{:S(2)}) async-start(), calls=%async_computation.11 | async-start | bytes 2359296 | tf_op jit(solution)/shard_map/reduce_scatter | solution.py:90
  71.3 38.5 %copy-start.6 = (bf16[1024,64]{0,1:T(8,128)(2,1)}, bf16[1024,64]{0,1:T(8,128)(2,1)S(1)}, u32[]{:S(2)}) copy-start(bf16[1024,64]{0,1:T(8,128)(2,1)S(1)} %fusion.66) | copy-start | bytes 393220
  112.8 40.3 %copy-start.1 = (bf16[1,128,1024]{2,1,0:T(8,128)(2,1)S(1)}, bf16[1,128,1024]{2,1,0:T(8,128)(2,1)}, u32[]{:S(2)}) copy-start(bf16[1,128,1024]{2,1,0:T(8,128)(2,1)} %param.15) | copy-start | bytes 786436
  112.8 70.3 %all-gather.16.cloned.1.call-start = ((), (), s32[]{:S(2)}) async-start(), calls=%async_computation.13 | async-start | bytes 1310720 | tf_op jit(solution)/shard_map/all_gather | solution.py:84
  113.6 99.3 %all-gather.14.cloned.1.call-start = ((), (), s32[]{:S(2)}) async-start(), calls=%async_computation.12 | async-start | bytes 2359296 | tf_op jit(solution)/shard_map/all_gather | solution.py:87
  154.2 288.8 %copy-start.22 = (f32[128]{0:T(128)}, f32[128]{0:T(128)S(1)}, u32[]{:S(2)}) copy-start(f32[128]{0:T(128)S(1)} %broadcast_multiply_fusion.4) | copy-start | bytes 1540
  155.4 287.6 %copy-start.25 = (f32[128]{0:T(128)}, f32[128]{0:T(128)S(1)}, u32[]{:S(2)}) copy-start(f32[128]{0:T(128)S(1)} %add_rsqrt_fusion) | copy-start | bytes 1540
  157.2 85.6 %all-gather.22.cloned.1.call-start = ((), (), s32[]{:S(2)}) async-start(), calls=%async_computation.22 | async-start | bytes 2359296 | tf_op jit(solution)/shard_map/all_gather | solution.py:87
  157.8 236.3 %all-gather.18.cloned.1.call-start = ((), (), s32[]{:S(2)}) async-start(), calls=%async_computation.14 | async-start | bytes 10485760 | tf_op jit(solution)/shard_map/all_gather | solution.py:84
  158.5 284.4 %reduce-scatter.15.cloned.1.call-start = ((), (), s32[]{:S(2)}) async-start(), calls=%async_computation.16 | async-start | bytes 2359296 | tf_op jit(solution)/shard_map/reduce_scatter | solution.py:90
  158.9 244.5 %copy-start.31 = (f32[512]{0:T(512)}, f32[512]{0:T(512)S(1)}, u32[]{:S(2)}) copy-start(f32[512]{0:T(512)S(1)} %dynamic_slice.34) | copy-start | bytes 6148
  403.4 84.1 %reduce-scatter.13.cloned.1.call-start = ((), (), s32[]{:S(2)}) async-start(), calls=%async_computation.15 | async-start | bytes 2359296 | tf_op jit(solution)/shard_map/reduce_scatter | solution.py:90
  408.1 79.4 %copy-start.5 = (bf16[1,128,1024]{2,1,0:T(8,128)(2,1)S(1)}, bf16[1,128,1024]{2,1,0:T(8,128)(2,1)}, u32[]{:S(2)}) copy-start(bf16[1,128,1024]{2,1,0:T(8,128)(2,1)} %param.29) | copy-start | bytes 786436
  408.1 110.3 %all-gather.20.cloned.1.call-start = ((), (), s32[]{:S(2)}) async-start(), calls=%async_computation.17 | async-start | bytes 2359296 | tf_op jit(solution)/shard_map/all_gather | solution.py:87
  490.4 82.3 %all-reduce.4.cloned.1.call-start = ((), (), s32[]{:S(2)}) async-start(), calls=%async_computation.23 | async-start | bytes 2097152
  494.6 106.8 %reduce-scatter.23.cloned.1.call-start = ((), (), s32[]{:S(2)}) async-start(), calls=%async_computation.21 | async-start | bytes 1310720 | tf_op jit(solution)/shard_map/reduce_scatter | solution.py:186
  499.3 126.5 %reduce-scatter.19.cloned.1.call-start = ((), (), s32[]{:S(2)}) async-start(), calls=%async_computation.19 | async-start | bytes 983040 | tf_op jit(solution)/shard_map/reduce_scatter | solution.py:191
  535.7 111.9 %reduce-scatter.21.cloned.1.call-start = ((), (), s32[]{:S(2)}) async-start(), calls=%async_computation.20 | async-start | bytes 327680 | tf_op jit(solution)/shard_map/reduce_scatter | solution.py:186
  538.5 151.7 %reduce-scatter.17.cloned.1.call-start = ((), (), s32[]{:S(2)}) async-start(), calls=%async_computation.18 | async-start | bytes 2359296 | tf_op jit(solution)/shard_map/reduce_scatter | solution.py:90
  542.6 36.3 %copy-start.30 = (f32[512]{0:T(512)S(1)}, f32[512]{0:T(512)}, u32[]{:S(2)}) copy-start(f32[512]{0:T(512)} %get-tuple-element.50) | copy-start | bytes 6148
  542.6 61.5 %copy-start.14 = (f32[1024]{0:T(1024)S(1)}, f32[1024]{0:T(1024)}, u32[]{:S(2)}) copy-start(f32[1024]{0:T(1024)} %get-tuple-element.14) | copy-start | bytes 12292
  542.6 61.6 %copy-start.13 = (f32[1024]{0:T(1024)S(1)}, f32[1024]{0:T(1024)}, u32[]{:S(2)}) copy-start(f32[1024]{0:T(1024)} %get-tuple-element.20) | copy-start | bytes 12292
  542.6 61.7 %copy-start.15 = (f32[1024]{0:T(1024)S(1)}, f32[1024]{0:T(1024)}, u32[]{:S(2)}) copy-start(f32[1024]{0:T(1024)} %get-tuple-element.26) | copy-start | bytes 12292
  575.0 28.2 %all-to-all-start.1 = ((bf16[8,32,512]{2,1,0:T(8,128)(2,1)}), bf16[8,32,512]{2,1,0:T(8,128)(2,1)S(1)}, u32[]{:S(2)}, u32[]{:S(2)}) async-start(bf16[8,32,512]{2,1,0:T(8,128)(2,1)} %dynamic-slice_bitcast_fusion), calls=%async_computation.7 | async-start | bytes 524288 | tf_op jit(solution)/shard_map/all_to_all | solution.py:192
  579.1 71.0 %copy-start.12 = (f32[4096]{0:T(1024)}, f32[4096]{0:T(1024)S(1)}, u32[]{:S(2)}) copy-start(f32[4096]{0:T(1024)S(1)} %dynamic_update_slice.11) | copy-start | bytes 49156
  604.1 86.1 %copy-start.21 = (f32[128]{0:T(128)S(1)}, f32[128]{0:T(128)}, u32[]{:S(2)}) copy-start(f32[128]{0:T(128)} %copy-done.20) | copy-start | bytes 1540
  604.1 86.1 %copy-start.24 = (f32[128]{0:T(128)S(1)}, f32[128]{0:T(128)}, u32[]{:S(2)}) copy-start(f32[128]{0:T(128)} %copy-done.23) | copy-start | bytes 1540
  625.8 23.2 %all-to-all-start = ((bf16[8,32,384]{2,1,0:T(8,128)(2,1)}), bf16[8,32,384]{2,1,0:T(8,128)(2,1)}, u32[]{:S(2)}, u32[]{:S(2)}) async-start(bf16[8,32,384]{2,1,0:T(8,128)(2,1)} %bitcast.168), calls=%async_computation.5 | async-start | bytes 393216 | tf_op jit(solution)/shard_map/all_to_all | solution.py:192
  (24 other events, 159.5 us)
Sparse Core Ops, SparseCore 0:
  33.3 28.9 all-gather.9
  63.8 45.9 all-gather.11
  113.1 39.9 reduce-scatter.10
  155.1 27.9 all-gather.15
  185.6 27.3 all-gather.13
  214.9 27.8 all-gather.21
  244.5 149.6 all-gather.17
  403.5 39.4 reduce-scatter.14
  446.3 41.1 reduce-scatter.12
  490.5 27.8 all-gather.19
  520.9 51.8 all-reduce.3
  574.9 26.5 reduce-scatter.22
  603.8 21.9 reduce-scatter.18
  628.6 18.8 reduce-scatter.20
  650.7 39.4 reduce-scatter.16
